TPU v7x, 512 devices: a whole 4x4x16 slice. The times are simulated.
512 devices in a mesh: walk: 8 (over x, core), param: 64 (over z, y).
Axes of the slice: x: 4, y: 4, z: 16, core: 2. Of those that a mesh axis runs over, the one named last changes fastest.
Arguments:
- jacobian: float32 [1024, 606208], P('walk', 'param'), may hold values from -0.16722973 to 0.16722973, as said below
- energies: float32 [1024], P('walk'), may hold values from -6 to 6
- shifts: float32 [8], replicated, may hold values from 1.6495989e-06 to 4.9487964e-05
Outputs:
- update: float32 [8, 606208], P(None, 'param')
Inputs may be any that keep to these rules, and one draw needn't show every extreme that they name: `jacobian`: Real-valued entries of both signs.
All inputs are finite; a program needn't handle non-finite values.
Results may differ from a plain program's by a relative error of at most 0.00028.
Values sent between devices are 32-bit elements; how exact they have to be, the bound alone decides.
A program may use at most 64 MiB of HBM per device.

v0:
```python
import jax
import jax.numpy as jnp
from jax import lax
from jax.sharding import PartitionSpec as P

ITERS = 3


highest = lax.Precision.HIGHEST
epsilon = 1e-06


def rows_dot(vectors, matrix):
    return lax.dot_general(
        vectors,
        matrix,
        (((1,), (1,)), ((), ())),
        precision=highest,
        preferred_element_type=jnp.float32,
    )


def project_sums(proj_part, mean_part):
    proj_total, mean_total = lax.psum((proj_part, mean_part), "param")
    return proj_total - mean_total[:, None]


def body(jacobian, energies, shifts):
    walker_rows, param_cols = jacobian.shape
    shift_count = shifts.shape[0]
    walkers = walker_rows * lax.axis_size("walk")
    total_params = param_cols * lax.axis_size("param")
    column_local = jnp.sum(jacobian, axis=0)
    column_total, energy_total = lax.psum((column_local, jnp.sum(energies)), "walk")
    column_mean = column_total / walkers
    energy_dev = energies - energy_total / walkers
    force_local = jnp.dot(
        energy_dev, jacobian, precision=highest, preferred_element_type=jnp.float32
    )
    gradient = lax.psum(force_local, "walk") / walkers
    residual = jnp.broadcast_to(gradient[None, :], (shift_count, param_cols))

    def single(values):
        return lax.psum(values, "param")

    solution = jnp.zeros_like(residual)
    direction = residual
    norm_now = single(jnp.sum(residual * residual, axis=1))
    for number in range(ITERS):
        proj_part = rows_dot(direction, jacobian)
        mean_part = jnp.dot(
            direction, column_mean, precision=highest, preferred_element_type=jnp.float32
        )
        centred = project_sums(proj_part, mean_part)
        back_terms = jnp.dot(
            centred, jacobian, precision=highest, preferred_element_type=jnp.float32
        )
        applied = lax.psum(back_terms, "walk") / walkers + shifts[:, None] * direction
        curvature = single(jnp.sum(direction * applied, axis=1))
        step_size = (norm_now / curvature)[:, None]
        solution = solution + step_size * direction
        residual = residual - step_size * applied
        if number + 1 < ITERS:
            norm_next = single(jnp.sum(residual * residual, axis=1))
            direction = residual + (norm_next / norm_now)[:, None] * direction
            norm_now = norm_next
    squares = single(jnp.sum(solution * solution, axis=1))
    norm_scale = lax.rsqrt(squares / total_params + epsilon)
    return solution * norm_scale[:, None]


def solution(mesh):
    return jax.shard_map(
        body,
        mesh=mesh,
        in_specs=(P("walk", "param"), P("walk"), P()),
        out_specs=P(None, "param"),
        check_vma=False,
    )
```

profile of v0, /device:TPU:8, one launch (start us, length us, event | category | flops | bytes accessed | tf_op | source)
XLA Modules:
  0.0 1645.1 jit_solution(16328389275141943479)
XLA Ops:
  6.5 0.0 copy-start.2
  6.5 0.0 all-reduce.16.cloned.1.call-start
  6.5 1.3 reduce_sum.83
  7.9 15.2 psum.133
  23.1 3.3 reduce_sum.86
  27.0 0.0 copy-done.2
  27.0 5.4 convolution_reduce_fusion
  32.4 0.0 all-reduce.16.cloned.1.call-update
  32.4 0.0 all-reduce.10.cloned.1.call-start
  32.5 73.1 %all-reduce.16.cloned.1.call-done = (f32[9472]{0:T(1024)}, f32[9472]{0:T(1024)}) async-done(((f32[9472]{0:T(1024)}, f32[9472]{0:T(1024)}), (f32[9472]{0:T(1024)}, f32[9472]{0:T(1024)})) %all-reduce.16.cloned.1.call-update) | async-done | bytes 75792 | tf_op jit(solution)/shard_map/psum | solution.py:40
  105.6 1.5 multiply_reduce_fusion.6
  107.1 0.0 copy-start.1
  107.1 5.8 fusion.6
  112.9 0.8 convolution_bitcast_fusion.2
  113.6 142.2 %all-reduce.3 = (f32[8,128]{1,0:T(8,128)S(1)}, f32[8]{0:T(128)S(1)}) all-reduce(f32[8,128]{1,0:T(8,128)S(1)} %fusion.6, f32[8]{0:T(128)S(1)} %convolution_bitcast_fusion.2), channel_id=1, replica_groups=mesh['walk'=8,'param'=64] {'param'}, use_global_device_ids=true, to_apply=%region_5.0 | all-reduce | flops 1032 | bytes 8256 | tf_op jit(solution)/shard_map/psum | solution.py:24
  255.9 5.5 fusion.12
  261.3 0.0 all-reduce.10.cloned.1.call-update
  261.4 0.0 all-reduce.12.cloned.1.call-start
  261.4 73.1 %all-reduce.10.cloned.1.call-done = f32[8,9472]{1,0:T(8,128)} async-done(((f32[8,9472]{1,0:T(8,128)}), f32[8,9472]{1,0:T(8,128)}) %all-reduce.10.cloned.1.call-update) | async-done | bytes 303120 | tf_op jit(solution)/shard_map/psum | solution.py:58
  334.5 0.0 copy-done.1
  334.5 1.2 multiply_reduce_fusion.5
  335.7 0.7 reduce_sum.85
  336.4 140.2 %all-reduce.2 = (f32[8]{0:T(128)S(1)}, f32[8]{0:T(128)S(1)}) all-reduce(f32[8]{0:T(128)S(1)} %reduce_sum.85, f32[8]{0:T(128)S(1)} %multiply_reduce_fusion.5), channel_id=1, replica_groups=mesh['walk'=8,'param'=64] {'param'}, use_global_device_ids=true, to_apply=%region_4.0 | all-reduce | flops 16 | bytes 128 | tf_op jit(solution)/shard_map/psum | solution.py:44
  476.6 1.2 multiply_reduce_fusion.4
  477.9 142.6 %psum.141 = f32[8]{0:T(128)S(1)} all-reduce(f32[8]{0:T(128)S(1)} %multiply_reduce_fusion.4), channel_id=1, replica_groups=mesh['walk'=8,'param'=64] {'param'}, use_global_device_ids=true, to_apply=%region_13.0 | all-reduce | flops 8 | bytes 64 | tf_op jit(solution)/shard_map/psum | solution.py:44
  620.5 1.8 convolution_bitcast_fusion.1
  622.3 0.0 copy-start
  622.3 6.4 fusion
  628.7 140.0 %all-reduce.1 = (f32[8,128]{1,0:T(8,128)S(1)}, f32[8]{0:T(128)S(1)}) all-reduce(f32[8,128]{1,0:T(8,128)S(1)} %fusion, f32[8]{0:T(128)S(1)} %convolution_bitcast_fusion.1), channel_id=1, replica_groups=mesh['walk'=8,'param'=64] {'param'}, use_global_device_ids=true, to_apply=%region_14.0 | all-reduce | flops 1032 | bytes 8256 | tf_op jit(solution)/shard_map/psum | solution.py:24
  768.8 5.5 fusion.10
  774.2 0.0 all-reduce.12.cloned.1.call-update
  774.3 0.0 all-reduce.14.cloned.1.call-start
  774.3 70.4 %all-reduce.12.cloned.1.call-done = f32[8,9472]{1,0:T(8,128)} async-done(((f32[8,9472]{1,0:T(8,128)}), f32[8,9472]{1,0:T(8,128)}) %all-reduce.12.cloned.1.call-update) | async-done | bytes 303120 | tf_op jit(solution)/shard_map/psum | solution.py:58
  844.7 0.0 copy-done
  844.7 1.3 multiply_reduce_fusion.3
  845.9 140.2 %psum.145 = f32[8]{0:T(128)S(1)} all-reduce(f32[8]{0:T(128)S(1)} %multiply_reduce_fusion.3), channel_id=1, replica_groups=mesh['walk'=8,'param'=64] {'param'}, use_global_device_ids=true, to_apply=%region_18.0 | all-reduce | flops 8 | bytes 64 | tf_op jit(solution)/shard_map/psum | solution.py:44
  986.1 1.3 multiply_reduce_fusion.2
  987.4 142.5 %psum.146 = f32[8]{0:T(128)S(1)} all-reduce(f32[8]{0:T(128)S(1)} %multiply_reduce_fusion.2), channel_id=1, replica_groups=mesh['walk'=8,'param'=64] {'param'}, use_global_device_ids=true, to_apply=%region_20.0 | all-reduce | flops 8 | bytes 64 | tf_op jit(solution)/shard_map/psum | solution.py:44
  1129.9 1.2 multiply_add_fusion.1
  1131.1 0.8 convolution_bitcast_fusion
  1131.8 5.8 fusion.20
  1137.6 140.0 %all-reduce = (f32[8,128]{1,0:T(8,128)S(1)}, f32[8]{0:T(128)S(1)}) all-reduce(f32[8,128]{1,0:T(8,128)S(1)} %fusion.20, f32[8]{0:T(128)S(1)} %convolution_bitcast_fusion), channel_id=1, replica_groups=mesh['walk'=8,'param'=64] {'param'}, use_global_device_ids=true, to_apply=%region_21.0 | all-reduce | flops 1032 | bytes 8256 | tf_op jit(solution)/shard_map/psum | solution.py:24
  1277.6 5.5 fusion.8
  1283.1 0.0 all-reduce.14.cloned.1.call-update
  1283.1 70.5 %all-reduce.14.cloned.1.call-done = f32[8,9472]{1,0:T(8,128)} async-done(((f32[8,9472]{1,0:T(8,128)}), f32[8,9472]{1,0:T(8,128)}) %all-reduce.14.cloned.1.call-update) | async-done | bytes 303120 | tf_op jit(solution)/shard_map/psum | solution.py:58
  1353.5 1.2 multiply_reduce_fusion.1
  1354.8 140.2 %psum.150 = f32[8]{0:T(128)S(1)} all-reduce(f32[8]{0:T(128)S(1)} %multiply_reduce_fusion.1), channel_id=1, replica_groups=mesh['walk'=8,'param'=64] {'param'}, use_global_device_ids=true, to_apply=%region_25.0 | all-reduce | flops 8 | bytes 64 | tf_op jit(solution)/shard_map/psum | solution.py:44
  1495.0 0.3 multiply_reduce_fusion
  1495.3 142.5 %psum.151 = f32[8]{0:T(128)S(1)} all-reduce(f32[8]{0:T(128)S(1)} %get-tuple-element.15), channel_id=1, replica_groups=mesh['walk'=8,'param'=64] {'param'}, use_global_device_ids=true, to_apply=%region_27.0 | all-reduce | flops 8 | bytes 64 | tf_op jit(solution)/shard_map/psum | solution.py:44
  1637.8 0.8 broadcast_multiply_fusion
  (7 shorter events, 0.1 us)
Async XLA Ops:
  6.5 20.5 %copy-start.2 = (f32[128]{0:T(128)S(1)}, f32[128]{0:T(128)}, u32[]{:S(2)}) copy-start(f32[128]{0:T(128)} %param.4) | copy-start | bytes 1540
  6.5 99.0 %all-reduce.16.cloned.1.call-start = ((), (), s32[]{:S(2)}) async-start(), calls=%async_computation.3 | async-start | bytes 163840 | tf_op jit(solution)/shard_map/psum | solution.py:40
  32.4 302.1 %all-reduce.10.cloned.1.call-start = ((), (), s32[]{:S(2)}) async-start(), calls=%async_computation | async-start | bytes 606208 | tf_op jit(solution)/shard_map/psum | solution.py:58
  107.1 227.4 %copy-start.1 = (f32[8]{0:T(128)S(1)}, f32[8]{0:T(128)}, u32[]{:S(2)}) copy-start(f32[8]{0:T(128)} %param.5) | copy-start | bytes 100
  261.4 583.3 %all-reduce.12.cloned.1.call-start = ((), (), s32[]{:S(2)}) async-start(), calls=%async_computation.1 | async-start | bytes 606208 | tf_op jit(solution)/shard_map/psum | solution.py:58
  622.3 222.4 %copy-start = (f32[8,9472]{1,0:T(8,128)S(1)}, f32[8,9472]{1,0:T(8,128)}, u32[]{:S(2)}) copy-start(f32[8,9472]{1,0:T(8,128)} %all-reduce.10.cloned.1.call-done) | copy-start | bytes 909316
  774.3 579.3 %all-reduce.14.cloned.1.call-start = ((), (), s32[]{:S(2)}) async-start(), calls=%async_computation.2 | async-start | bytes 606208 | tf_op jit(solution)/shard_map/psum | solution.py:58
Sparse Core Ops, SparseCore 0:
  32.5 73.0 all-reduce.15
  261.5 72.9 all-reduce.9
  774.4 70.2 all-reduce.11
  1283.2 70.2 all-reduce.13
where the time goes:
time: 1650 us
  blocking collectives  1290 us (78%)
  waiting for transfers between devices  287 us (17%)
  matrix products  43 us (3%)
    psum x6, blocking collectives, single(): return lax.psum(values, 'param')  848 us
    psum x3, blocking collectives, project_sums(): proj_total, mean_total = lax.psum((proj_part, mean_part), 'param')  422 us
    psum x3, waiting for transfers between devices, body(): lax.psum(back_terms, 'walk') / walkers + shifts[:, None] * direction  214 us
    psum x1, waiting for transfers between devices, body(): gradient = lax.psum(force_local, 'walk') / walkers  73.1 us
  transfers between devices with their start and end apart: 4, of which 4 were waited for; matrix products, arithmetic and copies ran while one was open for 0% of the time, Pallas kernels for 0%

commit v1 on v0

v1 whole, which is shorter than its diff:
```python
import functools

import jax
import jax.numpy as jnp
from jax import lax
from jax.experimental import pallas as pl
from jax.experimental.pallas import tpu as pltpu
from jax.sharding import PartitionSpec as P

EPSILON = 1e-06
LANE = 128
Y_SIZE = 4
MESH = pl.DeviceIdType.MESH


def lane_pick(row, lane, number):
    return jnp.sum(jnp.where(lane == number, row, 0.0), axis=1, keepdims=True)


def lane_pack(lane, values):
    row = jnp.zeros(lane.shape, jnp.float32)
    for number, value in enumerate(values):
        row = jnp.where(lane == number, value, row)
    return row


def dot_row(left, right):
    return jnp.sum(left * right, axis=1, keepdims=True)


def as_column(row):
    return jnp.transpose(jnp.broadcast_to(row, (LANE, LANE)))


def kernel(
    dims,
    jac_hbm, energy_ref, shift_ref, out_ref,
    jac, part0, part, got0, got, base, next1, next2,
    ybuf, zbuf, last, load_sem, walk_send, walk_recv, param_send, param_recv,
):
    nw, ny, nz, cols, blocks = dims
    width = blocks * LANE
    walkers = float(nw * LANE)
    params = float(ny * nz * cols)
    w = lax.axis_index("walk")
    p = lax.axis_index("param")
    y, z = lax.rem(p, ny), p // ny

    load = pltpu.make_async_copy(jac_hbm, jac.at[:, pl.ds(0, cols)], load_sem)
    load.start()

    barrier = pltpu.get_barrier_semaphore()

    def walk_peer(d):
        return (lax.rem(w + d, nw), p)

    def y_peer(d):
        return (w, z * ny + lax.rem(y + d, ny))

    def z_peer(d):
        return (w, lax.rem(z + d, nz) * ny + y)

    def each(count, step):
        def go(d, carry):
            step(d)
            return carry
        lax.fori_loop(1, count, go, 0)

    for count, peer in ((nw, walk_peer), (ny, y_peer), (nz, z_peer)):
        each(count, lambda d, peer=peer: pl.semaphore_signal(
            barrier, inc=1, device_id=peer(d), device_id_type=MESH))

    if nw * width > cols:
        jac[:, cols:] = jnp.zeros((LANE, nw * width - cols), jnp.float32)

    lane = lax.broadcasted_iota(jnp.int32, (1, LANE), 1)
    energy = energy_ref[...]
    group_mean = jnp.sum(energy, axis=1, keepdims=True) / float(LANE)
    energy_col = as_column(energy - group_mean)
    mean_row = jnp.broadcast_to(group_mean, (1, LANE))
    load.wait()

    def first_pass(k, carry):
        for b in range(blocks):
            block = jac[:, pl.ds(pl.multiple_of(k * width + b * LANE, LANE), LANE)]
            part0[k, :, b * LANE:(b + 1) * LANE] = jnp.sum(block * energy_col, axis=0, keepdims=True)
            part0[k, :, width + b * LANE:width + (b + 1) * LANE] = jnp.sum(block, axis=0, keepdims=True)
        part0[k, :, 2 * width:] = mean_row
        return carry
    lax.fori_loop(0, nw, first_pass, 0)

    pl.semaphore_wait(barrier, (nw - 1) + (ny - 1) + (nz - 1))

    def exchange(count, source, target, landed, send, recv, peer):
        def copy(d, dst):
            return pltpu.make_async_remote_copy(
                src_ref=source(d), dst_ref=dst, send_sem=send.at[d], recv_sem=recv.at[d],
                device_id=peer(d), device_id_type=MESH)
        each(count, lambda d: copy(d, target(d)).start())
        each(count, lambda d: copy(d, landed(d)).wait_recv())
        each(count, lambda d: copy(d, target(d)).wait_send())

    def scatter(number, pieces, buffer):
        exchange(nw, lambda d: pieces.at[lax.rem(w + d, nw)], lambda d: buffer.at[d], lambda d: buffer.at[d],
                 walk_send, walk_recv.at[number], walk_peer)

    def gather(number, buffer):
        exchange(nw, lambda d: buffer.at[w], lambda d: buffer.at[w], lambda d: buffer.at[lax.rem(w + nw - d, nw)],
                 walk_send, walk_recv.at[number], walk_peer)

    def param_sum(number, row):
        ys, zs = ybuf.at[number], zbuf.at[number]
        ys[0] = row
        exchange(ny, lambda d: ys.at[0], lambda d: ys.at[d], lambda d: ys.at[d],
                 param_send, param_recv.at[2 * number], y_peer)
        zs[0] = jnp.sum(ys[...], axis=0)
        exchange(nz, lambda d: zs.at[0], lambda d: zs.at[d], lambda d: zs.at[d],
                 param_send, param_recv.at[2 * number + 1], z_peer)
        return jnp.sum(zs[...], axis=0)

    scatter(0, part0, got0)
    own = part0[w]
    mean_total = own[:, 2 * width:]
    for d in range(1, nw):
        mean_total = mean_total + got0[d, :, 2 * width:]
    energy_mean = mean_total[:, :1] / float(nw)
    delta = own[:, 2 * width:2 * width + 1] - energy_mean
    column_sum = own[:, width:2 * width]
    force = own[:, :width] + delta * own[:, width:2 * width]
    dev_sum = delta
    for d in range(1, nw):
        delta = got0[d, :, 2 * width:2 * width + 1] - energy_mean
        piece = got0[d, :, width:2 * width]
        column_sum = column_sum + piece
        force = force + got0[d, :, :width] + delta * piece
        dev_sum = dev_sum + delta
    column_mean = column_sum / walkers
    base[w, :, :width] = (force - column_mean * (dev_sum * float(LANE))) / walkers
    base[w, :, width:] = column_mean
    gather(1, base)

    def project(vector, others):
        def step(k, carry):
            total, centre, dots = carry
            for b in range(blocks):
                row = vector[k, :, b * LANE:(b + 1) * LANE]
                block = jac[:, pl.ds(pl.multiple_of(k * width + b * LANE, LANE), LANE)]
                total = total + block * row
                centre = centre + base[k, :, width + b * LANE:width + (b + 1) * LANE] * row
                dots = tuple(
                    dot + other[k, :, b * LANE:(b + 1) * LANE] * row
                    for dot, other in zip(dots, others))
            return total, centre, dots
        zero = jnp.zeros((1, LANE), jnp.float32)
        total, centre, dots = lax.fori_loop(
            0, nw, step, (jnp.zeros((LANE, LANE), jnp.float32), zero, (zero,) * len(others)))
        row = jnp.sum(jnp.transpose(total), axis=0, keepdims=True)
        centre = jnp.sum(centre, axis=1, keepdims=True)
        dots = [jnp.sum(dot, axis=1, keepdims=True) for dot in dots]
        return jnp.concatenate([row - centre, lane_pack(lane, dots)], axis=1)

    def spread(weights, scalars):
        column = as_column(weights)

        def step(k, carry):
            for b in range(blocks):
                block = jac[:, pl.ds(pl.multiple_of(k * width + b * LANE, LANE), LANE)]
                part[k, :, b * LANE:(b + 1) * LANE] = jnp.sum(block * column, axis=0, keepdims=True)
            part[k, :, width:] = scalars
            return carry
        lax.fori_loop(0, nw, step, 0)

    def collect():
        total = part[w]
        for d in range(1, nw):
            total = total + got[d]
        return total[:, :width] / walkers, total[:, width:]

    seed_shift = shift_ref[0]

    reply = param_sum(0, project(base, (base,)))
    q0, m00 = reply[:, :LANE], lane_pick(reply[:, LANE:], lane, 0)
    spread(q0, lane_pack(lane, [dot_row(q0, q0)]))
    scatter(2, part, got)
    image, sums = collect()
    k00 = lane_pick(sums, lane, 0) / walkers
    r0 = base[w, :, :width]
    r1 = r0 - (m00 / (k00 + seed_shift * m00)) * (image + seed_shift * r0)
    next1[w] = r1
    gather(3, next1)

    reply = param_sum(1, project(next1, (next1, base)))
    q1, sums = reply[:, :LANE], reply[:, LANE:]
    m11, m01 = lane_pick(sums, lane, 0), lane_pick(sums, lane, 1)
    turn = m11 / m00
    p1 = q1 + turn * q0
    spread(p1, lane_pack(lane, [dot_row(q1, q1), dot_row(q0, q1), dot_row(p1, p1)]))
    scatter(4, part, got)
    image, sums = collect()
    k11, k01, pp1 = (lane_pick(sums, lane, i) / walkers for i in range(3))
    d1 = r1 + turn * r0
    dd1 = m11 + 2.0 * turn * m01 + turn * turn * m00
    next2[w] = r1 - (m11 / (pp1 + seed_shift * dd1)) * (image + seed_shift * d1)
    gather(5, next2)

    reply = param_sum(2, project(next2, (next2, base, next1)))
    q2, sums = reply[:, :LANE], reply[:, LANE:]
    m22, m02, m12 = (lane_pick(sums, lane, i) for i in range(3))
    last[0] = lane_pack(lane, [dot_row(q2, q2), dot_row(q0, q2), dot_row(q1, q2)])
    exchange(nw, lambda d: last.at[0], lambda d: last.at[d], lambda d: last.at[d],
             walk_send, walk_recv.at[6], walk_peer)
    sums = jnp.sum(last[...], axis=0)
    k22, k02, k12 = (lane_pick(sums, lane, i) / walkers for i in range(3))

    count = out_ref.shape[0]
    trial = lax.broadcasted_iota(jnp.int32, (count, LANE), 0)
    shift = jnp.zeros((count, LANE), jnp.float32)
    for number in range(count):
        shift = jnp.where(trial == number, shift_ref[number], shift)
    a00, a01, a02 = k00 + shift * m00, k01 + shift * m01, k02 + shift * m02
    a11, a12, a22 = k11 + shift * m11, k12 + shift * m12, k22 + shift * m22
    l10, l20 = a01 / a00, a02 / a00
    e1 = a11 - l10 * a01
    e21 = a12 - l20 * a01
    l21 = e21 / e1
    e2 = a22 - l20 * a02 - l21 * e21
    b1 = m01 - l10 * m00
    b2 = m02 - l20 * m00 - l21 * b1
    c2 = b2 / e2
    c1 = b1 / e1 - l21 * c2
    c0 = m00 / a00 - l10 * c1 - l20 * c2
    square = c0 * (c0 * m00 + 2.0 * (c1 * m01 + c2 * m02)) + c1 * (c1 * m11 + 2.0 * c2 * m12) + c2 * c2 * m22
    scale = lax.rsqrt(square / params + EPSILON)
    c0, c1, c2 = c0 * scale, c1 * scale, c2 * scale

    def write(k, b):
        at = slice(b * LANE, (b + 1) * LANE)
        out_ref[:, pl.ds(pl.multiple_of(k * width + b * LANE, LANE), LANE)] = (
            c0 * base[k, :, at] + c1 * next1[k, :, at] + c2 * next2[k, :, at])

    whole = cols // width

    def write_piece(k, carry):
        for b in range(blocks):
            write(k, b)
        return carry
    lax.fori_loop(0, whole, write_piece, 0)
    for b in range((cols - whole * width) // LANE):
        write(whole, b)


def solution(mesh):
    nw, npar = mesh.shape["walk"], mesh.shape["param"]
    ny = Y_SIZE
    nz = npar // ny

    def body(jacobian, energies, shifts):
        cols = jacobian.shape[1]
        blocks = -(-(cols // LANE) // nw)
        width = blocks * LANE
        count = shifts.shape[0]
        f32 = jnp.float32
        return pl.pallas_call(
            functools.partial(kernel, (nw, ny, nz, cols, blocks)),
            out_shape=jax.ShapeDtypeStruct((count, cols), f32),
            in_specs=[
                pl.BlockSpec(memory_space=pl.ANY),
                pl.BlockSpec(memory_space=pltpu.VMEM),
                pl.BlockSpec(memory_space=pltpu.SMEM),
            ],
            out_specs=pl.BlockSpec(memory_space=pltpu.VMEM),
            scratch_shapes=[
                pltpu.VMEM((LANE, nw * width), f32),
                pltpu.VMEM((nw, 1, 2 * width + LANE), f32),
                pltpu.VMEM((nw, 1, width + LANE), f32),
                pltpu.VMEM((nw, 1, 2 * width + LANE), f32),
                pltpu.VMEM((nw, 1, width + LANE), f32),
                pltpu.VMEM((nw, 1, 2 * width), f32),
                pltpu.VMEM((nw, 1, width), f32),
                pltpu.VMEM((nw, 1, width), f32),
                pltpu.VMEM((3, ny, 1, 2 * LANE), f32),
                pltpu.VMEM((3, nz, 1, 2 * LANE), f32),
                pltpu.VMEM((nw, 1, LANE), f32),
                pltpu.SemaphoreType.DMA,
                pltpu.SemaphoreType.DMA((nw,)),
                pltpu.SemaphoreType.DMA((7, nw)),
                pltpu.SemaphoreType.DMA((nz,)),
                pltpu.SemaphoreType.DMA((6, nz)),
            ],
            compiler_params=pltpu.CompilerParams(
                collective_id=0, has_side_effects=True, vmem_limit_bytes=48 << 20
            ),
        )(jacobian, energies.reshape(1, -1), shifts)

    return jax.shard_map(
        body,
        mesh=mesh,
        in_specs=(P("walk", "param"), P("walk"), P()),
        out_specs=P(None, "param"),
        check_vma=False,
    )
```

time: 1650 us -> 85 us (0.05)
  the two profiles are of different devices: /device:TPU:8 before, /device:TPU:1 now
where the time goes in v1:
time: 85 us; the launch traced here: 84.8 us
  Pallas kernels  80.4 us (95%)
  local copies, waits for them, and re-layouts  4.4 us (5%)
    pallas_call x1, Pallas kernels, body(): pl.pallas_call(functools.partial(kernel, (nw, ny, nz, cols, blocks)), out...  80.4 us
    unnamed x7, local copies, waits for them, and re-layouts  4.4 us

profile of v1, /device:TPU:1, one launch (start us, length us, event | category | flops | bytes accessed | tf_op | source)
XLA Modules:
  0.0 84.8 jit_solution(9146080590212521306)
XLA Ops:
  0.0 0.0 copy-start
  0.0 2.4 %copy-done = f32[128,9472]{1,0:T(8,128)S(1)} copy-done((f32[128,9472]{1,0:T(8,128)S(1)}, f32[128,9472]{1,0:T(8,128)}, u32[]{:S(2)}) %copy-start) | copy-done | bytes 4849688
  2.4 0.0 copy-start.1
  2.4 0.7 copy-done.1
  3.0 0.0 copy-start.2
  3.0 0.7 copy-done.2
  3.7 80.4 %shard_map.37 = f32[8,9472]{1,0:T(8,128)S(1)} custom-call(f32[128,9472]{1,0:T(8,128)S(1)} %copy-done, f32[1,128]{1,0:T(1,128)S(1)} %bitcast.1, f32[8]{0:T(128)S(1)} %copy-done.2), custom_call_target="tpu_custom_call" | custom-call | tf_op jit(solution)/shard_map/pallas_call | solution.py:263
  84.1 0.7 copy.5
Async XLA Ops:
  0.0 2.4 %copy-start = (f32[128,9472]{1,0:T(8,128)S(1)}, f32[128,9472]{1,0:T(8,128)}, u32[]{:S(2)}) copy-start(f32[128,9472]{1,0:T(8,128)} %jac_hbm.1) | copy-start | bytes 14548996
  2.4 0.7 copy-start.1
  3.0 0.7 copy-start.2

commit v2 on v1

--- a/solution.py
+++ b/solution.py
@@ -34,9 +34,10 @@
 
 def kernel(
     dims,
-    jac_hbm, energy_ref, shift_ref, out_ref,
-    jac, part0, part, got0, got, base, next1, next2,
-    ybuf, zbuf, last, load_sem, walk_send, walk_recv, param_send, param_recv,
+    jac_hbm, energy_hbm, shift_hbm, out_ref,
+    jac, energy_ref, shift_ref, part0, got0, base, next1, next2, full, sums_buf,
+    ybuf, zbuf, load_sem, walk_send, walk_recv, full_send, full_recv, small_send, small_recv,
+    param_send, param_recv,
 ):
     nw, ny, nz, cols, blocks = dims
     width = blocks * LANE
@@ -46,7 +47,11 @@
     p = lax.axis_index("param")
     y, z = lax.rem(p, ny), p // ny
 
-    load = pltpu.make_async_copy(jac_hbm, jac.at[:, pl.ds(0, cols)], load_sem)
+    load = pltpu.make_async_copy(jac_hbm, jac.at[:, pl.ds(0, cols)], load_sem.at[0])
+    load_energy = pltpu.make_async_copy(energy_hbm, energy_ref, load_sem.at[1])
+    load_shift = pltpu.make_async_copy(shift_hbm, shift_ref, load_sem.at[2])
+    load_energy.start()
+    load_shift.start()
     load.start()
 
     barrier = pltpu.get_barrier_semaphore()
@@ -74,6 +79,8 @@
         jac[:, cols:] = jnp.zeros((LANE, nw * width - cols), jnp.float32)
 
     lane = lax.broadcasted_iota(jnp.int32, (1, LANE), 1)
+    load_energy.wait()
+    load_shift.wait()
     energy = energy_ref[...]
     group_mean = jnp.sum(energy, axis=1, keepdims=True) / float(LANE)
     energy_col = as_column(energy - group_mean)
@@ -102,10 +109,6 @@
 
     def scatter(number, pieces, buffer):
         exchange(nw, lambda d: pieces.at[lax.rem(w + d, nw)], lambda d: buffer.at[d], lambda d: buffer.at[d],
-                 walk_send, walk_recv.at[number], walk_peer)
-
-    def gather(number, buffer):
-        exchange(nw, lambda d: buffer.at[w], lambda d: buffer.at[w], lambda d: buffer.at[lax.rem(w + nw - d, nw)],
                  walk_send, walk_recv.at[number], walk_peer)
 
     def param_sum(number, row):
@@ -137,79 +140,123 @@
     column_mean = column_sum / walkers
     base[w, :, :width] = (force - column_mean * (dev_sum * float(LANE))) / walkers
     base[w, :, width:] = column_mean
-    gather(1, base)
-
-    def project(vector, others):
-        def step(k, carry):
-            total, centre, dots = carry
-            for b in range(blocks):
-                row = vector[k, :, b * LANE:(b + 1) * LANE]
-                block = jac[:, pl.ds(pl.multiple_of(k * width + b * LANE, LANE), LANE)]
-                total = total + block * row
-                centre = centre + base[k, :, width + b * LANE:width + (b + 1) * LANE] * row
-                dots = tuple(
-                    dot + other[k, :, b * LANE:(b + 1) * LANE] * row
-                    for dot, other in zip(dots, others))
-            return total, centre, dots
-        zero = jnp.zeros((1, LANE), jnp.float32)
-        total, centre, dots = lax.fori_loop(
-            0, nw, step, (jnp.zeros((LANE, LANE), jnp.float32), zero, (zero,) * len(others)))
+
+    zero_row = jnp.zeros((1, LANE), jnp.float32)
+
+    def fresh(count):
+        return jnp.zeros((LANE, LANE), jnp.float32), zero_row, (zero_row,) * count
+
+    def project(k, carry, vector, others):
+        total, centre, dots = carry
+        for b in range(blocks):
+            at = slice(b * LANE, (b + 1) * LANE)
+            row = vector[k, :, at]
+            block = jac[:, pl.ds(pl.multiple_of(k * width + b * LANE, LANE), LANE)]
+            total = total + block * row
+            centre = centre + base[k, :, width + b * LANE:width + (b + 1) * LANE] * row
+            dots = tuple(dot + other[k, :, at] * row for dot, other in zip(dots, others))
+        return total, centre, dots
+
+    def message(carry):
+        total, centre, dots = carry
         row = jnp.sum(jnp.transpose(total), axis=0, keepdims=True)
         centre = jnp.sum(centre, axis=1, keepdims=True)
         dots = [jnp.sum(dot, axis=1, keepdims=True) for dot in dots]
         return jnp.concatenate([row - centre, lane_pack(lane, dots)], axis=1)
 
-    def spread(weights, scalars):
+    def spread(number, weights, scalars):
         column = as_column(weights)
+        small, large = sums_buf.at[number], full.at[number]
+        small[0] = lane_pack(lane, scalars)
+
+        def small_copy(d):
+            return pltpu.make_async_remote_copy(
+                src_ref=small.at[0], dst_ref=small.at[d], send_sem=small_send.at[number],
+                recv_sem=small_recv.at[number], device_id=walk_peer(d), device_id_type=MESH)
+        each(nw, lambda d: small_copy(d).start())
 
         def step(k, carry):
             for b in range(blocks):
                 block = jac[:, pl.ds(pl.multiple_of(k * width + b * LANE, LANE), LANE)]
-                part[k, :, b * LANE:(b + 1) * LANE] = jnp.sum(block * column, axis=0, keepdims=True)
-            part[k, :, width:] = scalars
+                large[k, 0, :, b * LANE:(b + 1) * LANE] = jnp.sum(block * column, axis=0, keepdims=True)
+            each(nw, lambda d: pltpu.make_async_remote_copy(
+                src_ref=large.at[k, 0], dst_ref=large.at[k, d], send_sem=full_send.at[number, k],
+                recv_sem=full_recv.at[number, k], device_id=walk_peer(d), device_id_type=MESH).start())
             return carry
         lax.fori_loop(0, nw, step, 0)
 
-    def collect():
-        total = part[w]
-        for d in range(1, nw):
-            total = total + got[d]
-        return total[:, :width] / walkers, total[:, width:]
+    def all_of(buffer, send, recv):
+        rest = buffer.at[pl.ds(1, nw - 1)]
+        return pltpu.make_async_remote_copy(
+            src_ref=rest, dst_ref=rest, send_sem=send, recv_sem=recv,
+            device_id=walk_peer(1), device_id_type=MESH)
+
+    def walk_sums(number):
+        whole = all_of(sums_buf.at[number], small_send.at[number], small_recv.at[number])
+        whole.wait_recv()
+        whole.wait_send()
+        return jnp.sum(sums_buf[number], axis=0)
+
+    def absorb(number, vector, advance, others):
+        def step(k, carry):
+            all_of(full.at[number, k], full_send.at[number, k], full_recv.at[number, k]).wait_recv()
+            image = jnp.sum(full[number, k], axis=0) / walkers
+            vector[k] = advance(k, image)
+            return project(k, carry, vector, others)
+        carry = lax.fori_loop(0, nw, step, fresh(len(others)))
+        for k in range(nw):
+            all_of(full.at[number, k], full_send.at[number, k], full_recv.at[number, k]).wait_send()
+        return message(carry)
 
     seed_shift = shift_ref[0]
 
-    reply = param_sum(0, project(base, (base,)))
+    def gather_copy(d, dst):
+        return pltpu.make_async_remote_copy(
+            src_ref=base.at[w], dst_ref=dst, send_sem=walk_send.at[d], recv_sem=walk_recv.at[1, d],
+            device_id=walk_peer(d), device_id_type=MESH)
+    each(nw, lambda d: gather_copy(d, base.at[w]).start())
+
+    def first_step(d, carry):
+        k = lax.rem(w + nw - d, nw)
+        gather_copy(d, base.at[k]).wait_recv()
+        return project(k, carry, base, (base,))
+    carry = lax.fori_loop(1, nw, first_step, project(w, fresh(1), base, (base,)))
+    each(nw, lambda d: gather_copy(d, base.at[w]).wait_send())
+
+    reply = param_sum(0, message(carry))
     q0, m00 = reply[:, :LANE], lane_pick(reply[:, LANE:], lane, 0)
-    spread(q0, lane_pack(lane, [dot_row(q0, q0)]))
-    scatter(2, part, got)
-    image, sums = collect()
-    k00 = lane_pick(sums, lane, 0) / walkers
-    r0 = base[w, :, :width]
-    r1 = r0 - (m00 / (k00 + seed_shift * m00)) * (image + seed_shift * r0)
-    next1[w] = r1
-    gather(3, next1)
-
-    reply = param_sum(1, project(next1, (next1, base)))
+    spread(0, q0, [dot_row(q0, q0)])
+    k00 = lane_pick(walk_sums(0), lane, 0) / walkers
+    step0 = m00 / (k00 + seed_shift * m00)
+
+    def advance0(k, image):
+        r0 = base[k, :, :width]
+        return r0 - step0 * (image + seed_shift * r0)
+
+    reply = param_sum(1, absorb(0, next1, advance0, (next1, base)))
     q1, sums = reply[:, :LANE], reply[:, LANE:]
     m11, m01 = lane_pick(sums, lane, 0), lane_pick(sums, lane, 1)
     turn = m11 / m00
     p1 = q1 + turn * q0
-    spread(p1, lane_pack(lane, [dot_row(q1, q1), dot_row(q0, q1), dot_row(p1, p1)]))
-    scatter(4, part, got)
-    image, sums = collect()
+    spread(1, p1, [dot_row(q1, q1), dot_row(q0, q1), dot_row(p1, p1)])
+    sums = walk_sums(1)
     k11, k01, pp1 = (lane_pick(sums, lane, i) / walkers for i in range(3))
-    d1 = r1 + turn * r0
     dd1 = m11 + 2.0 * turn * m01 + turn * turn * m00
-    next2[w] = r1 - (m11 / (pp1 + seed_shift * dd1)) * (image + seed_shift * d1)
-    gather(5, next2)
-
-    reply = param_sum(2, project(next2, (next2, base, next1)))
+    step1 = m11 / (pp1 + seed_shift * dd1)
+
+    def advance1(k, image):
+        r1 = next1[k]
+        return r1 - step1 * (image + seed_shift * (r1 + turn * base[k, :, :width]))
+
+    reply = param_sum(2, absorb(1, next2, advance1, (next2, base, next1)))
     q2, sums = reply[:, :LANE], reply[:, LANE:]
     m22, m02, m12 = (lane_pick(sums, lane, i) for i in range(3))
-    last[0] = lane_pack(lane, [dot_row(q2, q2), dot_row(q0, q2), dot_row(q1, q2)])
-    exchange(nw, lambda d: last.at[0], lambda d: last.at[d], lambda d: last.at[d],
-             walk_send, walk_recv.at[6], walk_peer)
-    sums = jnp.sum(last[...], axis=0)
+    small = sums_buf.at[2]
+    small[0] = lane_pack(lane, [dot_row(q2, q2), dot_row(q0, q2), dot_row(q1, q2)])
+    each(nw, lambda d: pltpu.make_async_remote_copy(
+        src_ref=small.at[0], dst_ref=small.at[d], send_sem=small_send.at[2],
+        recv_sem=small_recv.at[2], device_id=walk_peer(d), device_id_type=MESH).start())
+    sums = walk_sums(2)
     k22, k02, k12 = (lane_pick(sums, lane, i) / walkers for i in range(3))
 
     count = out_ref.shape[0]
@@ -265,30 +312,35 @@
             out_shape=jax.ShapeDtypeStruct((count, cols), f32),
             in_specs=[
                 pl.BlockSpec(memory_space=pl.ANY),
-                pl.BlockSpec(memory_space=pltpu.VMEM),
-                pl.BlockSpec(memory_space=pltpu.SMEM),
+                pl.BlockSpec(memory_space=pl.ANY),
+                pl.BlockSpec(memory_space=pl.ANY),
             ],
             out_specs=pl.BlockSpec(memory_space=pltpu.VMEM),
             scratch_shapes=[
                 pltpu.VMEM((LANE, nw * width), f32),
+                pltpu.VMEM((1, LANE), f32),
+                pltpu.SMEM((count,), f32),
                 pltpu.VMEM((nw, 1, 2 * width + LANE), f32),
-                pltpu.VMEM((nw, 1, width + LANE), f32),
                 pltpu.VMEM((nw, 1, 2 * width + LANE), f32),
-                pltpu.VMEM((nw, 1, width + LANE), f32),
                 pltpu.VMEM((nw, 1, 2 * width), f32),
                 pltpu.VMEM((nw, 1, width), f32),
                 pltpu.VMEM((nw, 1, width), f32),
+                pltpu.VMEM((2, nw, nw, 1, width), f32),
+                pltpu.VMEM((3, nw, 1, LANE), f32),
                 pltpu.VMEM((3, ny, 1, 2 * LANE), f32),
                 pltpu.VMEM((3, nz, 1, 2 * LANE), f32),
-                pltpu.VMEM((nw, 1, LANE), f32),
-                pltpu.SemaphoreType.DMA,
+                pltpu.SemaphoreType.DMA((3,)),
                 pltpu.SemaphoreType.DMA((nw,)),
-                pltpu.SemaphoreType.DMA((7, nw)),
+                pltpu.SemaphoreType.DMA((2, nw)),
+                pltpu.SemaphoreType.DMA((2, nw)),
+                pltpu.SemaphoreType.DMA((2, nw)),
+                pltpu.SemaphoreType.DMA((3,)),
+                pltpu.SemaphoreType.DMA((3,)),
                 pltpu.SemaphoreType.DMA((nz,)),
                 pltpu.SemaphoreType.DMA((6, nz)),
             ],
             compiler_params=pltpu.CompilerParams(
-                collective_id=0, has_side_effects=True, vmem_limit_bytes=48 << 20
+                collective_id=0, has_side_effects=True, vmem_limit_bytes=67043328
             ),
         )(jacobian, energies.reshape(1, -1), shifts)
 

time: 85 us -> 75 us (0.88)
  Pallas kernels: 80.4 us -> 73.1 us
  local copies, waits for them, and re-layouts: 4.4 us -> 1.7 us
    pallas_call x1, Pallas kernels: 80.4 us -> 73.1 us  [body(): pl.pallas_call(functools.partial(kernel, (nw, ny, nz, cols, blocks)), out...]
    unnamed x7 -> x1, local copies, waits for them, and re-layouts: 4.4 us -> 1.7 us
where the time goes in v2:
time: 75 us; the launch traced here: 74.8 us
  Pallas kernels  73.1 us (97%)
  local copies, waits for them, and re-layouts  1.7 us (2%)
    pallas_call x1, Pallas kernels, body(): pl.pallas_call(functools.partial(kernel, (nw, ny, nz, cols, blocks)), out...  73.1 us
    unnamed x1, local copies, waits for them, and re-layouts  1.7 us

profile of v2, /device:TPU:1, one launch (start us, length us, event | category | flops | bytes accessed | tf_op | source)
XLA Modules:
  0.0 74.8 jit_solution(169809437305400610)
XLA Ops:
  0.0 73.1 %shard_map.37 = f32[8,9472]{1,0:T(8,128)} custom-call(f32[128,9472]{1,0:T(8,128)} %jac_hbm.1, f32[1,128]{1,0:T(1,128)} %bitcast.1, f32[8]{0:T(128)} %shift_hbm.1), custom_call_target="tpu_custom_call" | custom-call | tf_op jit(solution)/shard_map/pallas_call | solution.py:310
  73.1 1.7 %copy.5 = f32[8,9472]{1,0:T(8,128)} copy(f32[8,9472]{1,0:T(8,128)} %shard_map.37) | data formatting | bytes 606208

commit v3 on v2

--- a/solution.py
+++ b/solution.py
@@ -36,7 +36,7 @@
     dims,
     jac_hbm, energy_hbm, shift_hbm, out_ref,
     jac, energy_ref, shift_ref, part0, got0, base, next1, next2, full, sums_buf,
-    ybuf, zbuf, load_sem, walk_send, walk_recv, full_send, full_recv, small_send, small_recv,
+    ybuf, zbuf, wide, load_sem, walk_send, walk_recv, full_send, full_recv, small_send, small_recv,
     param_send, param_recv,
 ):
     nw, ny, nz, cols, blocks = dims
@@ -111,14 +111,55 @@
         exchange(nw, lambda d: pieces.at[lax.rem(w + d, nw)], lambda d: buffer.at[d], lambda d: buffer.at[d],
                  walk_send, walk_recv.at[number], walk_peer)
 
+    def far_first(count):
+        return sorted(range(1, count), key=lambda d: -min(d, count - d))
+
+    def all_of(buffer, send, recv):
+        rest = buffer.at[pl.ds(1, buffer.shape[0] - 1)]
+        return pltpu.make_async_remote_copy(
+            src_ref=rest, dst_ref=rest, send_sem=send, recv_sem=recv,
+            device_id=walk_peer(1), device_id_type=MESH)
+
+    def spray(buffer, send, recv, count, peer):
+        for d in far_first(count):
+            pltpu.make_async_remote_copy(
+                src_ref=buffer.at[0], dst_ref=buffer.at[d], send_sem=send, recv_sem=recv,
+                device_id=peer(d), device_id_type=MESH).start()
+        return all_of(buffer, send, recv)
+
+    def direct_sum(number, row):
+        mine = wide.at[number - 1]
+        send, recv = param_send.at[number, 0], param_recv.at[number, 0]
+        mine[0] = row
+
+        def start(dz, dy):
+            pltpu.make_async_remote_copy(
+                src_ref=mine.at[0], dst_ref=mine.at[dz * ny + dy], send_sem=send, recv_sem=recv,
+                device_id=(w, lax.rem(z + dz, nz) * ny + lax.rem(y + dy, ny)), device_id_type=MESH).start()
+
+        def go(i, carry):
+            dz = nz // 2 + ((i + 1) // 2) * (1 - 2 * lax.rem(i, 2))
+            for dy in far_first(ny) + [0]:
+                start(dz, dy)
+            return carry
+        lax.fori_loop(0, nz - 1, go, 0)
+        for dy in far_first(ny):
+            start(0, dy)
+        whole = all_of(mine, send, recv)
+        whole.wait_recv()
+        whole.wait_send()
+        return jnp.sum(mine[...], axis=0)
+
     def param_sum(number, row):
         ys, zs = ybuf.at[number], zbuf.at[number]
         ys[0] = row
-        exchange(ny, lambda d: ys.at[0], lambda d: ys.at[d], lambda d: ys.at[d],
-                 param_send, param_recv.at[2 * number], y_peer)
+        first = spray(ys, param_send.at[number, 0], param_recv.at[number, 0], ny, y_peer)
+        first.wait_recv()
         zs[0] = jnp.sum(ys[...], axis=0)
-        exchange(nz, lambda d: zs.at[0], lambda d: zs.at[d], lambda d: zs.at[d],
-                 param_send, param_recv.at[2 * number + 1], z_peer)
+        second = spray(zs, param_send.at[number, 1], param_recv.at[number, 1], nz, z_peer)
+        first.wait_send()
+        second.wait_recv()
+        second.wait_send()
         return jnp.sum(zs[...], axis=0)
 
     scatter(0, part0, got0)
@@ -185,12 +226,6 @@
             return carry
         lax.fori_loop(0, nw, step, 0)
 
-    def all_of(buffer, send, recv):
-        rest = buffer.at[pl.ds(1, nw - 1)]
-        return pltpu.make_async_remote_copy(
-            src_ref=rest, dst_ref=rest, send_sem=send, recv_sem=recv,
-            device_id=walk_peer(1), device_id_type=MESH)
-
     def walk_sums(number):
         whole = all_of(sums_buf.at[number], small_send.at[number], small_recv.at[number])
         whole.wait_recv()
@@ -233,7 +268,7 @@
         r0 = base[k, :, :width]
         return r0 - step0 * (image + seed_shift * r0)
 
-    reply = param_sum(1, absorb(0, next1, advance0, (next1, base)))
+    reply = direct_sum(1, absorb(0, next1, advance0, (next1, base)))
     q1, sums = reply[:, :LANE], reply[:, LANE:]
     m11, m01 = lane_pick(sums, lane, 0), lane_pick(sums, lane, 1)
     turn = m11 / m00
@@ -248,7 +283,7 @@
         r1 = next1[k]
         return r1 - step1 * (image + seed_shift * (r1 + turn * base[k, :, :width]))
 
-    reply = param_sum(2, absorb(1, next2, advance1, (next2, base, next1)))
+    reply = direct_sum(2, absorb(1, next2, advance1, (next2, base, next1)))
     q2, sums = reply[:, :LANE], reply[:, LANE:]
     m22, m02, m12 = (lane_pick(sums, lane, i) for i in range(3))
     small = sums_buf.at[2]
@@ -329,6 +364,7 @@
                 pltpu.VMEM((3, nw, 1, LANE), f32),
                 pltpu.VMEM((3, ny, 1, 2 * LANE), f32),
                 pltpu.VMEM((3, nz, 1, 2 * LANE), f32),
+                pltpu.VMEM((2, ny * nz, 1, 2 * LANE), f32),
                 pltpu.SemaphoreType.DMA((3,)),
                 pltpu.SemaphoreType.DMA((nw,)),
                 pltpu.SemaphoreType.DMA((2, nw)),
@@ -336,8 +372,8 @@
                 pltpu.SemaphoreType.DMA((2, nw)),
                 pltpu.SemaphoreType.DMA((3,)),
                 pltpu.SemaphoreType.DMA((3,)),
-                pltpu.SemaphoreType.DMA((nz,)),
-                pltpu.SemaphoreType.DMA((6, nz)),
+                pltpu.SemaphoreType.DMA((3, 2)),
+                pltpu.SemaphoreType.DMA((3, 2)),
             ],
             compiler_params=pltpu.CompilerParams(
                 collective_id=0, has_side_effects=True, vmem_limit_bytes=67043328

time: 75 us -> 70.2 us (0.936)
  Pallas kernels: 73.1 us -> 68.3 us
    pallas_call x1, Pallas kernels: 73.1 us -> 68.3 us  [body(): pl.pallas_call(functools.partial(kernel, (nw, ny, nz, cols, blocks)), out...]
where the time goes in v3:
time: 70.2 us; the launch traced here: 70 us
  Pallas kernels  68.3 us (97%)
  local copies, waits for them, and re-layouts  1.7 us (2%)
    pallas_call x1, Pallas kernels, body(): pl.pallas_call(functools.partial(kernel, (nw, ny, nz, cols, blocks)), out...  68.3 us
    unnamed x1, local copies, waits for them, and re-layouts  1.7 us

profile of v3, /device:TPU:1, one launch (start us, length us, event | category | flops | bytes accessed | tf_op | source)
XLA Modules:
  0.0 70.0 jit_solution(553040233127356282)
XLA Ops:
  0.0 68.3 %shard_map.37 = f32[8,9472]{1,0:T(8,128)} custom-call(f32[128,9472]{1,0:T(8,128)} %jac_hbm.1, f32[1,128]{1,0:T(1,128)} %bitcast.1, f32[8]{0:T(128)} %shift_hbm.1), custom_call_target="tpu_custom_call" | custom-call | tf_op jit(solution)/shard_map/pallas_call | solution.py:345
  68.3 1.7 %copy.5 = f32[8,9472]{1,0:T(8,128)} copy(f32[8,9472]{1,0:T(8,128)} %shard_map.37) | data formatting | bytes 606208

commit v4 on v3

--- a/solution.py
+++ b/solution.py
@@ -35,9 +35,9 @@
 def kernel(
     dims,
     jac_hbm, energy_hbm, shift_hbm, out_ref,
-    jac, energy_ref, shift_ref, part0, got0, base, next1, next2, full, sums_buf,
+    jac, energy_ref, shift_ref, part0, got0, base, next1, next2, image_buf, full, sums_buf,
     ybuf, zbuf, wide, load_sem, walk_send, walk_recv, full_send, full_recv, small_send, small_recv,
-    param_send, param_recv,
+    param_send, param_recv, hello,
 ):
     nw, ny, nz, cols, blocks = dims
     width = blocks * LANE
@@ -47,12 +47,19 @@
     p = lax.axis_index("param")
     y, z = lax.rem(p, ny), p // ny
 
-    load = pltpu.make_async_copy(jac_hbm, jac.at[:, pl.ds(0, cols)], load_sem.at[0])
-    load_energy = pltpu.make_async_copy(energy_hbm, energy_ref, load_sem.at[1])
-    load_shift = pltpu.make_async_copy(shift_hbm, shift_ref, load_sem.at[2])
+    load_energy = pltpu.make_async_copy(energy_hbm, energy_ref, load_sem.at[nw])
+    load_shift = pltpu.make_async_copy(shift_hbm, shift_ref, load_sem.at[nw + 1])
+    filled = cols // width
+
+    def load(k, size):
+        to = pl.ds(pl.multiple_of(k * width, LANE), size)
+        return pltpu.make_async_copy(jac_hbm.at[:, to], jac.at[:, to], load_sem.at[k])
+
+    loads = [load(k, min(width, cols - k * width)) for k in range(nw) if k * width < cols]
     load_energy.start()
     load_shift.start()
-    load.start()
+    for copy in loads:
+        copy.start()
 
     barrier = pltpu.get_barrier_semaphore()
 
@@ -85,16 +92,23 @@
     group_mean = jnp.sum(energy, axis=1, keepdims=True) / float(LANE)
     energy_col = as_column(energy - group_mean)
     mean_row = jnp.broadcast_to(group_mean, (1, LANE))
-    load.wait()
-
-    def first_pass(k, carry):
+
+    def first_pass(k):
         for b in range(blocks):
             block = jac[:, pl.ds(pl.multiple_of(k * width + b * LANE, LANE), LANE)]
             part0[k, :, b * LANE:(b + 1) * LANE] = jnp.sum(block * energy_col, axis=0, keepdims=True)
             part0[k, :, width + b * LANE:width + (b + 1) * LANE] = jnp.sum(block, axis=0, keepdims=True)
         part0[k, :, 2 * width:] = mean_row
+
+    def first_full(k, carry):
+        load(k, width).wait()
+        first_pass(k)
         return carry
-    lax.fori_loop(0, nw, first_pass, 0)
+    lax.fori_loop(0, filled, first_full, 0)
+    for k in range(filled, nw):
+        if k < len(loads):
+            loads[k].wait()
+        first_pass(k)
 
     pl.semaphore_wait(barrier, (nw - 1) + (ny - 1) + (nz - 1))
 
@@ -127,10 +141,12 @@
                 device_id=peer(d), device_id_type=MESH).start()
         return all_of(buffer, send, recv)
 
-    def direct_sum(number, row):
-        mine = wide.at[number - 1]
+    def param_sum(number, carry):
+        total, centre, dots = carry
+        row = jnp.sum(jnp.transpose(total), axis=0, keepdims=True)
+        mine, ys, zs = wide.at[number], ybuf.at[number], zbuf.at[number]
         send, recv = param_send.at[number, 0], param_recv.at[number, 0]
-        mine[0] = row
+        mine[0] = row - jnp.sum(centre, axis=1, keepdims=True)
 
         def start(dz, dy):
             pltpu.make_async_remote_copy(
@@ -145,22 +161,25 @@
         lax.fori_loop(0, nz - 1, go, 0)
         for dy in far_first(ny):
             start(0, dy)
+        ys[0] = lane_pack(lane, [jnp.sum(dot, axis=1, keepdims=True) for dot in dots])
+        first = spray(ys, param_send.at[number, 1], param_recv.at[number, 1], ny, y_peer)
+        first.wait_recv()
+        zs[0] = jnp.sum(ys[...], axis=0)
+        spray(zs, param_send.at[number, 2], param_recv.at[number, 2], nz, z_peer)
+        first.wait_send()
         whole = all_of(mine, send, recv)
         whole.wait_recv()
         whole.wait_send()
         return jnp.sum(mine[...], axis=0)
 
-    def param_sum(number, row):
-        ys, zs = ybuf.at[number], zbuf.at[number]
-        ys[0] = row
-        first = spray(ys, param_send.at[number, 0], param_recv.at[number, 0], ny, y_peer)
-        first.wait_recv()
-        zs[0] = jnp.sum(ys[...], axis=0)
-        second = spray(zs, param_send.at[number, 1], param_recv.at[number, 1], nz, z_peer)
-        first.wait_send()
-        second.wait_recv()
-        second.wait_send()
-        return jnp.sum(zs[...], axis=0)
+    def param_dots(number):
+        whole = all_of(zbuf.at[number], param_send.at[number, 2], param_recv.at[number, 2])
+        whole.wait_recv()
+        whole.wait_send()
+        return jnp.sum(zbuf[number], axis=0)
+
+    for d in far_first(ny):
+        pl.semaphore_signal(hello, inc=1, device_id=y_peer(d), device_id_type=MESH)
 
     scatter(0, part0, got0)
     own = part0[w]
@@ -198,13 +217,6 @@
             dots = tuple(dot + other[k, :, at] * row for dot, other in zip(dots, others))
         return total, centre, dots
 
-    def message(carry):
-        total, centre, dots = carry
-        row = jnp.sum(jnp.transpose(total), axis=0, keepdims=True)
-        centre = jnp.sum(centre, axis=1, keepdims=True)
-        dots = [jnp.sum(dot, axis=1, keepdims=True) for dot in dots]
-        return jnp.concatenate([row - centre, lane_pack(lane, dots)], axis=1)
-
     def spread(number, weights, scalars):
         column = as_column(weights)
         small, large = sums_buf.at[number], full.at[number]
@@ -241,7 +253,7 @@
         carry = lax.fori_loop(0, nw, step, fresh(len(others)))
         for k in range(nw):
             all_of(full.at[number, k], full_send.at[number, k], full_recv.at[number, k]).wait_send()
-        return message(carry)
+        return carry
 
     seed_shift = shift_ref[0]
 
@@ -258,40 +270,43 @@
     carry = lax.fori_loop(1, nw, first_step, project(w, fresh(1), base, (base,)))
     each(nw, lambda d: gather_copy(d, base.at[w]).wait_send())
 
-    reply = param_sum(0, message(carry))
-    q0, m00 = reply[:, :LANE], lane_pick(reply[:, LANE:], lane, 0)
+    pl.semaphore_wait(hello, ny - 1)
+    q0 = param_sum(0, carry)
     spread(0, q0, [dot_row(q0, q0)])
+    m00 = lane_pick(param_dots(0), lane, 0)
     k00 = lane_pick(walk_sums(0), lane, 0) / walkers
     step0 = m00 / (k00 + seed_shift * m00)
 
     def advance0(k, image):
         r0 = base[k, :, :width]
+        image_buf[k] = image
         return r0 - step0 * (image + seed_shift * r0)
 
-    reply = direct_sum(1, absorb(0, next1, advance0, (next1, base)))
-    q1, sums = reply[:, :LANE], reply[:, LANE:]
+    q1 = param_sum(1, absorb(0, next1, advance0, (next1, base)))
+    spread(1, q1, [dot_row(q1, q1), dot_row(q0, q1)])
+    sums = param_dots(1)
     m11, m01 = lane_pick(sums, lane, 0), lane_pick(sums, lane, 1)
     turn = m11 / m00
-    p1 = q1 + turn * q0
-    spread(1, p1, [dot_row(q1, q1), dot_row(q0, q1), dot_row(p1, p1)])
     sums = walk_sums(1)
-    k11, k01, pp1 = (lane_pick(sums, lane, i) / walkers for i in range(3))
-    dd1 = m11 + 2.0 * turn * m01 + turn * turn * m00
+    k11, k01 = (lane_pick(sums, lane, i) / walkers for i in range(2))
+    pp1 = k11 + turn * (2.0 * k01 + turn * k00)
+    dd1 = m11 + turn * (2.0 * m01 + turn * m00)
     step1 = m11 / (pp1 + seed_shift * dd1)
 
     def advance1(k, image):
         r1 = next1[k]
-        return r1 - step1 * (image + seed_shift * (r1 + turn * base[k, :, :width]))
-
-    reply = direct_sum(2, absorb(1, next2, advance1, (next2, base, next1)))
-    q2, sums = reply[:, :LANE], reply[:, LANE:]
-    m22, m02, m12 = (lane_pick(sums, lane, i) for i in range(3))
+        direction = r1 + turn * base[k, :, :width]
+        return r1 - step1 * (image + turn * image_buf[k] + seed_shift * direction)
+
+    q2 = param_sum(2, absorb(1, next2, advance1, (next2, base, next1)))
     small = sums_buf.at[2]
     small[0] = lane_pack(lane, [dot_row(q2, q2), dot_row(q0, q2), dot_row(q1, q2)])
     each(nw, lambda d: pltpu.make_async_remote_copy(
         src_ref=small.at[0], dst_ref=small.at[d], send_sem=small_send.at[2],
         recv_sem=small_recv.at[2], device_id=walk_peer(d), device_id_type=MESH).start())
     sums = walk_sums(2)
+    dots = param_dots(2)
+    m22, m02, m12 = (lane_pick(dots, lane, i) for i in range(3))
     k22, k02, k12 = (lane_pick(sums, lane, i) / walkers for i in range(3))
 
     count = out_ref.shape[0]
@@ -360,20 +375,22 @@
                 pltpu.VMEM((nw, 1, 2 * width), f32),
                 pltpu.VMEM((nw, 1, width), f32),
                 pltpu.VMEM((nw, 1, width), f32),
+                pltpu.VMEM((nw, 1, width), f32),
                 pltpu.VMEM((2, nw, nw, 1, width), f32),
                 pltpu.VMEM((3, nw, 1, LANE), f32),
-                pltpu.VMEM((3, ny, 1, 2 * LANE), f32),
-                pltpu.VMEM((3, nz, 1, 2 * LANE), f32),
-                pltpu.VMEM((2, ny * nz, 1, 2 * LANE), f32),
-                pltpu.SemaphoreType.DMA((3,)),
+                pltpu.VMEM((3, ny, 1, LANE), f32),
+                pltpu.VMEM((3, nz, 1, LANE), f32),
+                pltpu.VMEM((3, ny * nz, 1, LANE), f32),
+                pltpu.SemaphoreType.DMA((nw + 2,)),
                 pltpu.SemaphoreType.DMA((nw,)),
                 pltpu.SemaphoreType.DMA((2, nw)),
                 pltpu.SemaphoreType.DMA((2, nw)),
                 pltpu.SemaphoreType.DMA((2, nw)),
                 pltpu.SemaphoreType.DMA((3,)),
                 pltpu.SemaphoreType.DMA((3,)),
-                pltpu.SemaphoreType.DMA((3, 2)),
-                pltpu.SemaphoreType.DMA((3, 2)),
+                pltpu.SemaphoreType.DMA((3, 3)),
+                pltpu.SemaphoreType.DMA((3, 3)),
+                pltpu.SemaphoreType.REGULAR,
             ],
             compiler_params=pltpu.CompilerParams(
                 collective_id=0, has_side_effects=True, vmem_limit_bytes=67043328

time: 70.2 us -> 68.2 us (0.972)
  Pallas kernels: 68.3 us -> 66.4 us
    pallas_call x1, Pallas kernels: 68.3 us -> 66.4 us  [body(): pl.pallas_call(functools.partial(kernel, (nw, ny, nz, cols, blocks)), out...]
where the time goes in v4:
time: 68.2 us; the launch traced here: 68.1 us
  Pallas kernels  66.4 us (97%)
  local copies, waits for them, and re-layouts  1.7 us (2%)
    pallas_call x1, Pallas kernels, body(): pl.pallas_call(functools.partial(kernel, (nw, ny, nz, cols, blocks)), out...  66.4 us
    unnamed x1, local copies, waits for them, and re-layouts  1.7 us

profile of v4, /device:TPU:1, one launch (start us, length us, event | category | flops | bytes accessed | tf_op | source)
XLA Modules:
  0.0 68.1 jit_solution(5799679728047240336)
XLA Ops:
  0.0 66.4 %shard_map.37 = f32[8,9472]{1,0:T(8,128)} custom-call(f32[128,9472]{1,0:T(8,128)} %jac_hbm.1, f32[1,128]{1,0:T(1,128)} %bitcast.1, f32[8]{0:T(128)} %shift_hbm.1), custom_call_target="tpu_custom_call" | custom-call | tf_op jit(solution)/shard_map/pallas_call | solution.py:360
  66.4 1.7 %copy.5 = f32[8,9472]{1,0:T(8,128)} copy(f32[8,9472]{1,0:T(8,128)} %shard_map.37) | data formatting | bytes 606208

commit v5 on v4

--- a/solution.py
+++ b/solution.py
@@ -112,21 +112,25 @@
 
     pl.semaphore_wait(barrier, (nw - 1) + (ny - 1) + (nz - 1))
 
+    def far_first(count):
+        return sorted(range(1, count), key=lambda d: -min(d, count - d))
+
+    def each_far(count, step):
+        for d in far_first(count):
+            step(d)
+
     def exchange(count, source, target, landed, send, recv, peer):
         def copy(d, dst):
             return pltpu.make_async_remote_copy(
                 src_ref=source(d), dst_ref=dst, send_sem=send.at[d], recv_sem=recv.at[d],
                 device_id=peer(d), device_id_type=MESH)
-        each(count, lambda d: copy(d, target(d)).start())
+        each_far(count, lambda d: copy(d, target(d)).start())
         each(count, lambda d: copy(d, landed(d)).wait_recv())
         each(count, lambda d: copy(d, target(d)).wait_send())
 
     def scatter(number, pieces, buffer):
         exchange(nw, lambda d: pieces.at[lax.rem(w + d, nw)], lambda d: buffer.at[d], lambda d: buffer.at[d],
                  walk_send, walk_recv.at[number], walk_peer)
-
-    def far_first(count):
-        return sorted(range(1, count), key=lambda d: -min(d, count - d))
 
     def all_of(buffer, send, recv):
         rest = buffer.at[pl.ds(1, buffer.shape[0] - 1)]
@@ -226,13 +230,13 @@
             return pltpu.make_async_remote_copy(
                 src_ref=small.at[0], dst_ref=small.at[d], send_sem=small_send.at[number],
                 recv_sem=small_recv.at[number], device_id=walk_peer(d), device_id_type=MESH)
-        each(nw, lambda d: small_copy(d).start())
+        each_far(nw, lambda d: small_copy(d).start())
 
         def step(k, carry):
             for b in range(blocks):
                 block = jac[:, pl.ds(pl.multiple_of(k * width + b * LANE, LANE), LANE)]
                 large[k, 0, :, b * LANE:(b + 1) * LANE] = jnp.sum(block * column, axis=0, keepdims=True)
-            each(nw, lambda d: pltpu.make_async_remote_copy(
+            each_far(nw, lambda d: pltpu.make_async_remote_copy(
                 src_ref=large.at[k, 0], dst_ref=large.at[k, d], send_sem=full_send.at[number, k],
                 recv_sem=full_recv.at[number, k], device_id=walk_peer(d), device_id_type=MESH).start())
             return carry
@@ -261,7 +265,7 @@
         return pltpu.make_async_remote_copy(
             src_ref=base.at[w], dst_ref=dst, send_sem=walk_send.at[d], recv_sem=walk_recv.at[1, d],
             device_id=walk_peer(d), device_id_type=MESH)
-    each(nw, lambda d: gather_copy(d, base.at[w]).start())
+    each_far(nw, lambda d: gather_copy(d, base.at[w]).start())
 
     def first_step(d, carry):
         k = lax.rem(w + nw - d, nw)
@@ -301,7 +305,7 @@
     q2 = param_sum(2, absorb(1, next2, advance1, (next2, base, next1)))
     small = sums_buf.at[2]
     small[0] = lane_pack(lane, [dot_row(q2, q2), dot_row(q0, q2), dot_row(q1, q2)])
-    each(nw, lambda d: pltpu.make_async_remote_copy(
+    each_far(nw, lambda d: pltpu.make_async_remote_copy(
         src_ref=small.at[0], dst_ref=small.at[d], send_sem=small_send.at[2],
         recv_sem=small_recv.at[2], device_id=walk_peer(d), device_id_type=MESH).start())
     sums = walk_sums(2)

time: 68.2 us -> 67.4 us (0.988)
  Pallas kernels: 66.4 us -> 65.5 us
    pallas_call x1, Pallas kernels: 66.4 us -> 65.5 us  [body(): pl.pallas_call(functools.partial(kernel, (nw, ny, nz, cols, blocks)), out...]
where the time goes in v5:
time: 67.4 us; the launch traced here: 67.2 us
  Pallas kernels  65.5 us (97%)
  local copies, waits for them, and re-layouts  1.7 us (3%)
    pallas_call x1, Pallas kernels, body(): pl.pallas_call(functools.partial(kernel, (nw, ny, nz, cols, blocks)), out...  65.5 us
    unnamed x1, local copies, waits for them, and re-layouts  1.7 us

profile of v5, /device:TPU:1, one launch (start us, length us, event | category | flops | bytes accessed | tf_op | source)
XLA Modules:
  0.0 67.2 jit_solution(5665748556436433310)
XLA Ops:
  0.0 65.5 %shard_map.37 = f32[8,9472]{1,0:T(8,128)} custom-call(f32[128,9472]{1,0:T(8,128)} %jac_hbm.1, f32[1,128]{1,0:T(1,128)} %bitcast.1, f32[8]{0:T(128)} %shift_hbm.1), custom_call_target="tpu_custom_call" | custom-call | tf_op jit(solution)/shard_map/pallas_call | solution.py:364
  65.5 1.7 %copy.5 = f32[8,9472]{1,0:T(8,128)} copy(f32[8,9472]{1,0:T(8,128)} %shard_map.37) | data formatting | bytes 606208

commit v6 on v5

--- a/solution.py
+++ b/solution.py
@@ -162,7 +162,9 @@
             for dy in far_first(ny) + [0]:
                 start(dz, dy)
             return carry
-        lax.fori_loop(0, nz - 1, go, 0)
+        for dz in far_first(nz):
+            for dy in far_first(ny) + [0]:
+                start(dz, dy)
         for dy in far_first(ny):
             start(0, dy)
         ys[0] = lane_pack(lane, [jnp.sum(dot, axis=1, keepdims=True) for dot in dots])

time: 67.4 us -> 67.2 us (level)
  no operation moved by 1% of the time
where the time goes in v6:
time: 67.2 us; the launch traced here: 67.1 us
  Pallas kernels  65.3 us (97%)
  local copies, waits for them, and re-layouts  1.7 us (3%)
    pallas_call x1, Pallas kernels, body(): pl.pallas_call(functools.partial(kernel, (nw, ny, nz, cols, blocks)), out...  65.3 us
    unnamed x1, local copies, waits for them, and re-layouts  1.7 us

profile of v6, /device:TPU:1, one launch (start us, length us, event | category | flops | bytes accessed | tf_op | source)
XLA Modules:
  0.0 67.1 jit_solution(7918355155087861722)
XLA Ops:
  0.0 65.3 %shard_map.37 = f32[8,9472]{1,0:T(8,128)} custom-call(f32[128,9472]{1,0:T(8,128)} %jac_hbm.1, f32[1,128]{1,0:T(1,128)} %bitcast.1, f32[8]{0:T(128)} %shift_hbm.1), custom_call_target="tpu_custom_call" | custom-call | tf_op jit(solution)/shard_map/pallas_call | solution.py:366
  65.4 1.7 %copy.5 = f32[8,9472]{1,0:T(8,128)} copy(f32[8,9472]{1,0:T(8,128)} %shard_map.37) | data formatting | bytes 606208
